TPU v7x, 32 devices: a whole 2x2x4 slice. The times are simulated.
32 devices in a mesh: groups: 2 (over y), cells: 8 (over z, x), freq: 2 (over core).
Axes of the slice: x: 2, y: 2, z: 4, core: 2. Of those that a mesh axis runs over, the one named last changes fastest.
Arguments:
- adjoint: float32 [2, 256], P(None, ('groups', 'cells')), parts along dimension 1, may hold values from -6 to 6
- target_x: float32 [256], P(('groups', 'cells')), parts along dimension 0, may hold values from 0 to 1024
- target_y: float32 [256], P(('groups', 'cells')), parts along dimension 0, may hold values from 0 to 8
- target_z: float32 [256], P(('groups', 'cells')), parts along dimension 0, may hold values from 256 to 512
- assignment: int32 [256], P(('groups', 'cells')), parts along dimension 0, may hold values from 0 to 63
- level_codes: int32 [16384], P(('groups', 'cells', 'freq')), parts along dimension 0, may hold values from 0 to 15
- cell_params: bfloat16 [8, 16384], P(None, ('groups', 'cells', 'freq')), parts along dimension 1, may hold values from -5 to 5
- level_table: bfloat16 [16, 256], replicated, may hold values from -4 to 4
- w_proj: bfloat16 [8, 256], replicated, may hold values from -2 to 2
- w_one: bfloat16 [256, 256], replicated, may hold values from -0.375 to 0.375
- b_one: float32 [256], replicated, may hold values from -3 to 3
- w_two: bfloat16 [256, 256], replicated, may hold values from -0.375 to 0.375
- b_two: float32 [256], replicated, may hold values from -3 to 3
- w_out: bfloat16 [256, 128], replicated, may hold values from -0.375 to 0.375
Outputs:
- grad_out: float32 [512, 128], P('groups'), parts along dimension 0
- grad_w2: float32 [512, 256], P('groups'), parts along dimension 0
- grad_b2: float32 [512], P('groups'), parts along dimension 0
- grad_w1: float32 [512, 256], P('groups'), parts along dimension 0
- grad_b1: float32 [512], P('groups'), parts along dimension 0
- grad_table: float32 [32, 256], P('groups'), parts along dimension 0
- grad_proj: float32 [16, 256], P('groups'), parts along dimension 0
- grad_params: float32 [8, 16384], P(None, ('groups', 'cells', 'freq')), parts along dimension 1
There are 2 independent parts, one for each index of `groups`. A program takes and returns all parts, laid end to end along the dimension named above; an argument that names none is the same for every part. Nothing has to cross between parts.
All inputs are finite; a program needn't handle non-finite values.
Results may differ from a plain program's by a relative error of at most 0.01.
Values may be sent and summed in bfloat16 or wider, within the bound.
A program may use at most 64 MiB of HBM per device.

v0:
```python
import math

import jax
import jax.numpy as jnp
from jax import lax
from jax.sharding import PartitionSpec as P

SIDE = 1024


wave_low = 1.0
wave_high = 3.0
kernel_gain = 150.0


def silu_slope(value):
    sigma = jax.nn.sigmoid(value)
    return sigma * (1.0 + value * (1.0 - sigma))


def contract(left, right, left_dim, right_dim):
    return lax.dot_general(
        left, right, (((left_dim,), (right_dim,)), ((), ())), preferred_element_type=jnp.float32
    )


def kernel_tile(point_x, point_y, point_z, freq_value, cell_col, cell_row, count_freq):
    wave = wave_low + (wave_high - wave_low) * freq_value / (count_freq - 1)
    offset_x = point_x[:, None] - cell_col[None, :]
    offset_y = point_y[:, None] - cell_row[None, :]
    square = offset_x * offset_x + offset_y * offset_y + (point_z * point_z)[:, None]
    distance = jnp.sqrt(square)
    amplitude = kernel_gain * point_z[:, None] / square
    phase = wave[:, None] * distance
    return (
        (amplitude * jnp.cos(phase)).astype(jnp.bfloat16),
        (amplitude * jnp.sin(phase)).astype(jnp.bfloat16),
    )


def forward_pass(level_codes, cell_params, level_table, w_proj, w_one, b_one, w_two, b_two):
    levels = level_table.shape[0]
    onehot = (level_codes[:, None] == jnp.arange(levels, dtype=jnp.int32)[None, :]).astype(
        jnp.bfloat16
    )
    hidden_in = (
        jnp.dot(onehot, level_table, preferred_element_type=jnp.float32)
        + contract(cell_params, w_proj, 0, 0)
    ).astype(jnp.bfloat16)
    pre_one = jnp.dot(hidden_in, w_one, preferred_element_type=jnp.float32) + b_one
    act_one = jax.nn.silu(pre_one).astype(jnp.bfloat16)
    pre_two = jnp.dot(act_one, w_two, preferred_element_type=jnp.float32) + b_two
    act_two = jax.nn.silu(pre_two).astype(jnp.bfloat16)
    return (onehot, hidden_in, pre_one, act_one, pre_two, act_two)


def upper_grads(spectra, w_out, act_one, pre_two, act_two):
    back_two = contract(spectra, w_out, 0, 1)
    delta_two = (back_two * silu_slope(pre_two)).astype(jnp.bfloat16)
    grad_out = contract(act_two, spectra, 0, 1)
    grad_w2 = contract(act_one, delta_two, 0, 0)
    grad_b2 = jnp.sum(delta_two.astype(jnp.float32), axis=0)
    return ((grad_out, grad_w2, grad_b2), delta_two)


def lower_grads(delta_two, w_two, w_one, pre_one, hidden_in, onehot, cell_params, w_proj):
    back_one = contract(delta_two, w_two, 1, 1)
    delta_one = (back_one * silu_slope(pre_one)).astype(jnp.bfloat16)
    grad_w1 = contract(hidden_in, delta_one, 0, 0)
    grad_b1 = jnp.sum(delta_one.astype(jnp.float32), axis=0)
    back_zero = contract(delta_one, w_one, 1, 1).astype(jnp.bfloat16)
    grad_table = contract(onehot, back_zero, 0, 0)
    grad_proj = contract(cell_params, back_zero, 1, 0)
    grad_params = contract(w_proj, back_zero, 1, 1)
    return ((grad_w1, grad_b1, grad_table, grad_proj), grad_params)


def body(
    adjoint,
    target_x,
    target_y,
    target_z,
    assignment,
    level_codes,
    cell_params,
    level_table,
    w_proj,
    w_one,
    b_one,
    w_two,
    b_two,
    w_out,
):
    cell_count = level_codes.shape[0]
    freq_count = w_out.shape[1] // 2
    freq_size = lax.axis_size("freq")
    cell_rank = lax.axis_index("cells")
    freq_rank = lax.axis_index("freq")
    first_cell = (cell_rank * freq_size + freq_rank) * cell_count
    index = first_cell + jnp.arange(cell_count, dtype=jnp.int32)
    cell_col = (index % SIDE).astype(jnp.float32)
    cell_row = (index // SIDE).astype(jnp.float32)
    freq_grid = jnp.arange(freq_count, dtype=jnp.int32).astype(jnp.float32)
    stacked = jnp.concatenate(
        [
            adjoint,
            target_x[None, :],
            target_y[None, :],
            target_z[None, :],
            assignment.astype(jnp.float32)[None, :],
        ],
        axis=0,
    )
    initial = jnp.zeros((2 * freq_count, cell_count), jnp.float32)
    total = initial
    piece = lax.all_gather(stacked, "cells", axis=1, tiled=True)
    length = piece.shape[1]
    block_len = math.gcd(length, 256)
    sections = piece.reshape(6, length // block_len, block_len).transpose(1, 0, 2)

    def inner(accum, rows):
        adj_round = rows[0:2].astype(jnp.bfloat16)
        kre, kim = kernel_tile(rows[2], rows[3], rows[4], rows[5], cell_col, cell_row, freq_count)
        select = (rows[5][:, None] == freq_grid[None, :]).astype(jnp.bfloat16)
        part_a = select * adj_round[0][:, None]
        part_b = select * adj_round[1][:, None]
        left_re = jnp.concatenate([part_a, part_b], axis=1)
        left_im = jnp.concatenate([part_b, -part_a], axis=1)
        return (accum + contract(left_re, kre, 0, 0) + contract(left_im, kim, 0, 0), None)

    total, unused = lax.scan(inner, total, sections)
    local_spec = total.astype(jnp.bfloat16)
    scale = 1.0 / math.sqrt(cell_count * lax.axis_size("cells") * freq_size)
    onehot, hidden_in, pre_one, act_one, pre_two, act_two = forward_pass(
        level_codes, cell_params, level_table, w_proj, w_one, b_one, w_two, b_two
    )
    upper, delta_two = upper_grads(local_spec, w_out, act_one, pre_two, act_two)
    lower, grad_params = lower_grads(
        delta_two, w_two, w_one, pre_one, hidden_in, onehot, cell_params, w_proj
    )
    totals = lax.psum(
        (
            upper[0] * scale,
            upper[1] * scale,
            upper[2] * scale,
            lower[0] * scale,
            lower[1] * scale,
            lower[2] * scale,
            lower[3] * scale,
        ),
        ("cells", "freq"),
    )
    grad_out, grad_w2, grad_b2, grad_w1, grad_b1, grad_table, grad_proj = totals
    return (grad_out, grad_w2, grad_b2, grad_w1, grad_b1, grad_table, grad_proj, grad_params)


def solution(mesh):
    placed = (
        P(None, ("groups", "cells")),
        P(("groups", "cells")),
        P(("groups", "cells")),
        P(("groups", "cells")),
        P(("groups", "cells")),
        P(("groups", "cells", "freq")),
        P(None, ("groups", "cells", "freq")),
        P(),
        P(),
        P(),
        P(),
        P(),
        P(),
        P(),
    )
    return jax.shard_map(
        body,
        mesh=mesh,
        in_specs=placed,
        out_specs=(
            P("groups", None),
            P("groups", None),
            P("groups"),
            P("groups", None),
            P("groups"),
            P("groups", None),
            P("groups", None),
            P(None, ("groups", "cells", "freq")),
        ),
        check_vma=False,
    )
```

profile of v0, /device:TPU:0, one launch (start us, length us, event | category | flops | bytes accessed | tf_op | source)
XLA Modules:
  0.0 153.7 jit_solution(16663212163118805640)
XLA Ops:
  7.2 0.0 copy-start
  7.2 0.0 all-reduce.4.cloned.1.call-start
  7.2 0.0 copy-start.15
  7.3 0.7 copy-done.15
  7.9 0.0 copy-start.10
  7.9 0.6 copy-done.11
  8.6 0.0 copy-done.12
  8.6 0.0 copy-done.8
  8.6 0.0 copy-done.10
  8.7 32.4 %all-gather = f32[8,16,6]{1,2,0:T(8,128)S(1)} all-gather(f32[1,16,6]{1,2,0:T(8,128)S(1)} %bitcast.55), channel_id=1, replica_groups=mesh['groups'=2,'cells'=8,'freq'=2] {'cells'}, dimensions={0}, use_global_device_ids=true | all-gather | bytes 3456 | tf_op jit(solution)/shard_map/all_gather | solution.py:116
  41.1 0.1 reshape.88
  41.2 0.1 fusion.35
  41.4 1.2 fusion.7
  42.6 0.0 copy-start.6
  42.6 0.0 copy-start.7
  42.6 1.2 fusion.3
  43.8 0.0 copy-done.6
  43.9 0.0 copy-done.7
  43.9 0.0 copy-start.4
  43.9 0.0 copy-start.5
  43.9 0.3 fusion.6
  44.2 0.4 copy-done.4
  44.6 0.0 copy-done.5
  44.6 0.3 fusion
  44.9 0.6 copy-done.1
  45.5 0.0 copy-done.9
  45.5 0.2 convolution_add_fusion.2
  45.7 0.0 copy-done
  45.7 0.4 copy-done.14
  46.2 0.3 convolution_add_fusion.1
  46.4 0.0 copy-start.13
  46.4 1.0 convolution_multiply_fusion.4
  47.4 0.0 copy-done.13
  47.4 0.3 convert_reduce_fusion.1
  47.8 1.0 convolution_multiply_fusion.3
  48.8 0.3 convert_reduce_fusion
  49.1 1.0 convolution_multiply_fusion.2
  50.1 0.0 all-reduce.4.cloned.1.call-update
  50.2 0.3 convolution_convert_fusion
  50.4 0.1 fusion.4
  50.6 0.3 convolution_multiply_fusion.5
  50.9 57.9 %all-reduce = (f32[256]{0:T(256)}, f32[256]{0:T(256)}, f32[16,256]{1,0:T(8,128)}, f32[8,256]{1,0:T(8,128)}) all-reduce(f32[256]{0:T(256)S(1)} %broadcast_multiply_fusion.1, f32[256]{0:T(256)S(1)} %broadcast_multiply_fusion, ...), channel_id=1, replica_groups=mesh['groups'=2,'cells'=8,'freq'=2] {'cells','freq'}, use_global_device_ids=true, to_apply=%region_3.4 | all-reduce | flops 6656 | bytes 53248 | tf_op jit(solution)/shard_map/psum | solution.py:141
  108.7 0.8 convolution_bitcast_fusion
  109.5 34.0 %all-reduce.4.cloned.1.call-done = (f32[256,128]{1,0:T(8,128)}, f32[256,256]{1,0:T(8,128)}, f32[256,256]{1,0:T(8,128)}) async-done(((f32[256,128]{1,0:T(8,128)}, f32[256,256]{1,0:T(8,128)}, f32[256,256]{1,0:T(8,128)}), (f32[256,128]{1,0:T(8,128)}, f32[256,256]{1,0:T(8,128)}, f32[256,256]{1,0:T(8,128)})) %all-reduce.4.cloned.1.call-update) | async-done | bytes 655376 | tf_op jit(solution)/shard_map/psum | solution.py:141
  143.5 1.6 %copy.27 = f32[256,128]{1,0:T(8,128)} copy(f32[256,128]{1,0:T(8,128)} %get-tuple-element.49) | data formatting | bytes 262144
  145.1 0.7 copy.28
  145.8 0.3 copy-done.2
  146.2 0.7 copy.29
  (20 shorter events, 0.1 us)
Async XLA Ops:
  7.2 38.5 %copy-start = (bf16[256,256]{1,0:T(8,128)(2,1)S(1)}, bf16[256,256]{1,0:T(8,128)(2,1)}, u32[]{:S(2)}) copy-start(bf16[256,256]{1,0:T(8,128)(2,1)} %param.25) | copy-start | bytes 393220
  7.2 136.3 %all-reduce.4.cloned.1.call-start = ((), (), s32[]{:S(2)}) async-start(), calls=%async_computation | async-start | bytes 1310720 | tf_op jit(solution)/shard_map/psum | solution.py:141
  7.2 0.7 copy-start.15
  7.9 0.7 copy-start.11
  7.9 0.7 copy-start.12
  7.9 0.7 copy-start.8
  7.9 0.7 copy-start.10
  42.6 1.3 copy-start.6
  42.6 1.3 copy-start.7
  43.9 0.7 copy-start.4
  43.9 0.7 copy-start.5
  44.6 0.9 copy-start.1
  44.6 0.9 copy-start.9
  45.5 0.7 copy-start.14
  46.4 1.0 copy-start.13
  143.5 1.6 %copy-start.3 = (f32[256,256]{1,0:T(8,128)S(1)}, f32[256,256]{1,0:T(8,128)}, u32[]{:S(2)}) copy-start(f32[256,256]{1,0:T(8,128)} %get-tuple-element.50) | copy-start | bytes 786436
  145.1 1.0 copy-start.2
Sparse Core Ops, SparseCore 0:
  50.3 93.1 all-reduce.3
where the time goes:
time: 154 us
  blocking collectives  90.3 us (59%)
  waiting for transfers between devices  34 us (22%)
  between operations  14.2 us (9%)
  matrix products  8.64 us (6%)
  local copies, waits for them, and re-layouts  6.34 us (4%)
    psum x1, blocking collectives, body(): lax.psum((upper[0] * scale, upper[1] * scale, upper[2] * scale, lower[0]...  57.9 us
    psum x1, waiting for transfers between devices, body(): lax.psum((upper[0] * scale, upper[1] * scale, upper[2] * scale, lower[0]...  34 us
    all_gather x1, blocking collectives, body(): piece = lax.all_gather(stacked, 'cells', axis=1, tiled=True)  32.4 us
    dot_general x12, matrix products, contract(): lax.dot_general(left, right, (((left_dim,), (right_dim,)), ((), ())), pre...  7.85 us
    unnamed x36, local copies, waits for them, and re-layouts  6.31 us
  transfers between devices with their start and end apart: 1, of which 1 were waited for; matrix products, arithmetic and copies ran while one was open for 1% of the time, Pallas kernels for 0%

commit v1 on v0

v1 whole, which is shorter than its diff:
```python
import functools
import math

import jax
import jax.numpy as jnp
from jax import lax
from jax.experimental import pallas as pl
from jax.experimental.pallas import tpu as pltpu
from jax.sharding import PartitionSpec as P

SIDE = 1024
LANES = 128
WIRE = jnp.bfloat16
WIRE_ROWS = 16

wave_low = 1.0
wave_high = 3.0
kernel_gain = 150.0

f32 = jnp.float32
bf16 = jnp.bfloat16


def contract(left, right, left_dim, right_dim):
    return lax.dot_general(
        left, right, (((left_dim,), (right_dim,)), ((), ())), preferred_element_type=f32
    )


def sin_cos(phase):
    turns = jnp.floor(phase * (2.0 / math.pi) + 0.5)
    rest = phase - turns * 1.5703125
    rest = rest - turns * 4.837512969970703125e-4
    rest = rest - turns * 7.54978995489188216e-8
    square = rest * rest
    sine = rest + rest * square * (
        -1.6666654611e-1 + square * (8.3321608736e-3 + square * -1.9515295891e-4)
    )
    cosine = (
        1.0
        - 0.5 * square
        + square
        * square
        * (4.166664568298827e-2 + square * (-1.388731625493765e-3 + square * 2.443315711809948e-5))
    )
    quarter = turns.astype(jnp.int32)
    odd = (quarter & 1) == 1
    sin_part = jnp.where(odd, cosine, sine)
    cos_part = jnp.where(odd, sine, cosine)
    sin_part = jnp.where((quarter & 2) == 2, -sin_part, sin_part)
    cos_part = jnp.where(((quarter + 1) & 2) == 2, -cos_part, cos_part)
    return sin_part, cos_part


def each(count, step):
    if count <= 16:
        for k in range(1, count):
            step(k)
    else:

        @pl.loop(1, count)
        def _(k):
            step(k)


def kernel(
    dims,
    adj_ref,
    x_ref,
    y_ref,
    z_ref,
    asg_ref,
    codes_ref,
    params_ref,
    table_ref,
    proj_ref,
    w1_ref,
    b1_ref,
    w2_ref,
    b2_ref,
    wo_ref,
    go_ref,
    gw2_ref,
    gb2_ref,
    gw1_ref,
    gb1_ref,
    gt_ref,
    gp_ref,
    gc_ref,
    gath,
    feat,
    hid,
    act1,
    slope1,
    act2,
    slope2,
    spec,
    d2,
    d1,
    part_a,
    part_b,
    cs_a,
    cs_b,
    cr_a,
    cr_b,
    rs_a,
    rs_b,
    rr_a,
    rr_b,
    ag_a,
    ag_b,
    g_send,
    g_recv,
    c_send,
    c_recv,
    rs_send_a,
    rs_recv_a,
    rs_send_b,
    rs_recv_b,
    ag_send_a,
    ag_recv_a,
    ag_send_b,
    ag_recv_b,
    fw_send_a,
    fw_recv_a,
    fw_send_b,
    fw_recv_b,
):
    n, nf, per, piece_a, piece_b, scale = dims
    me = lax.axis_index("cells")
    core = lax.axis_index("freq")
    other = 1 - core
    cells = codes_ref.shape[1]
    local = x_ref.shape[1]
    hidden = w1_ref.shape[0]
    half = hidden // nf
    levels = table_ref.shape[0]
    n_par = proj_ref.shape[0]
    outs = wo_ref.shape[1]
    freqs = outs // 2

    def peer(k):
        return {"cells": lax.rem(me + k, n)}

    def source(k):
        return lax.rem(me + n - k, n)

    mate = {"freq": other}

    def remote(src, dst, send, recv, device):
        return pltpu.make_async_remote_copy(
            src_ref=src,
            dst_ref=dst,
            send_sem=send,
            recv_sem=recv,
            device_id=device,
            device_id_type=pl.DeviceIdType.MESH,
        )

    barrier = pltpu.get_barrier_semaphore()
    each(
        n,
        lambda k: pl.semaphore_signal(
            barrier, inc=1, device_id=peer(k), device_id_type=pl.DeviceIdType.MESH
        ),
    )
    pl.semaphore_signal(barrier, inc=1, device_id=mate, device_id_type=pl.DeviceIdType.MESH)

    width = per * local
    rows = jnp.concatenate(
        [
            adj_ref[...],
            x_ref[...],
            y_ref[...],
            z_ref[...],
            asg_ref[...].astype(f32),
            jnp.zeros((2, local), f32),
        ],
        axis=0,
    )
    spread = jnp.concatenate([rows] * per, axis=1)
    lane = lax.broadcasted_iota(jnp.int32, (8, width), 1)
    start = lax.rem(me, per) * local
    inside = jnp.logical_and(lane >= start, lane < start + local)
    gath[me] = jnp.where(inside, spread, 0.0)

    codes = codes_ref[...]
    onehot = (
        jnp.where(codes == lax.broadcasted_iota(jnp.int32, (levels, cells), 0), 1.0, 0.0)
    ).astype(bf16)
    feat[0:levels, :] = onehot
    hid[...] = (
        contract(onehot, table_ref[...], 0, 0) + contract(params_ref[...], proj_ref[...], 0, 0)
    ).astype(bf16)
    pre = contract(hid[...], w1_ref[...], 1, 0) + b1_ref[...]
    sig = 1.0 / (1.0 + jnp.exp(-pre))
    act1[...] = (pre * sig).astype(bf16)
    slope1[...] = sig * (1.0 + pre * (1.0 - sig))

    pl.semaphore_wait(barrier, n)

    def gather_copy(k):
        return remote(gath.at[me], gath.at[me], g_send.at[k], g_recv.at[k], peer(k))

    each(n, lambda k: gather_copy(k).start())

    pre = contract(act1[...], w2_ref[...], 1, 0) + b2_ref[...]
    sig = 1.0 / (1.0 + jnp.exp(-pre))
    act2[...] = (pre * sig).astype(bf16)
    slope2[...] = sig * (1.0 + pre * (1.0 - sig))

    each(n, lambda k: gather_copy(k).wait())

    index = (me * nf + core) * cells + lax.broadcasted_iota(jnp.int32, (cells, width), 0)
    cell_col = (index % SIDE).astype(f32)
    cell_row = (index // SIDE).astype(f32)
    line = lax.broadcasted_iota(jnp.int32, (outs, width), 0)
    upper = line < freqs
    freq_line = jnp.where(upper, line, line - freqs).astype(f32)

    def section(first):
        block = gath[first]
        for j in range(1, per):
            block = block + gath[first + j]
        adj = block[0:2].astype(bf16).astype(f32)
        a0, a1 = adj[0:1], adj[1:2]
        px, py, pz, pf = block[2:3], block[3:4], block[4:5], block[5:6]
        wave = wave_low + (wave_high - wave_low) * pf / (freqs - 1)
        off_x = px - cell_col
        off_y = py - cell_row
        square = off_x * off_x + off_y * off_y + pz * pz
        distance = jnp.sqrt(square)
        amplitude = (kernel_gain * pz) / square
        sine, cosine = sin_cos(wave * distance)
        kre = (amplitude * cosine).astype(bf16)
        kim = (amplitude * sine).astype(bf16)
        chosen = freq_line == pf
        left_re = jnp.where(chosen, jnp.where(upper, a0, a1), 0.0).astype(bf16)
        left_im = jnp.where(chosen, jnp.where(upper, a1, -a0), 0.0).astype(bf16)
        return contract(kre, left_re, 1, 1) + contract(kim, left_im, 1, 1)

    if n == per:
        total = section(0)
    else:
        total = lax.fori_loop(
            0,
            n // per,
            lambda i, acc: acc + section(i * per),
            jnp.zeros((cells, outs), f32),
        )
    spec[...] = total.astype(bf16)

    delta2 = (contract(spec[...], wo_ref[...], 1, 1) * slope2[...]).astype(bf16)
    d2[...] = delta2
    grad_b2 = jnp.sum(delta2.astype(f32), axis=0, keepdims=True)
    grad = contract(act2[...], spec[...], 0, 0)
    for c in range(nf):
        part_a[c, 0:half, :] = grad[c * half : (c + 1) * half]
    grad = contract(act1[...], d2[...], 0, 0)
    for c in range(nf):
        part_a[c, half : half + hidden, :] = grad[:, c * half : (c + 1) * half]
    used_a = half + hidden
    if used_a < n * piece_a:
        part_a[:, used_a:, :] = jnp.zeros((nf, n * piece_a - used_a, half), f32)
    cs_a[...] = part_a[other].astype(WIRE)
    mate_a = remote(cs_a, cr_a, c_send.at[0], c_recv.at[0], mate)
    mate_a.start()

    delta1 = (contract(d2[...], w2_ref[...], 1, 1) * slope1[...]).astype(bf16)
    d1[...] = delta1
    grad_b1 = jnp.sum(delta1.astype(f32), axis=0, keepdims=True)

    def span(k, piece):
        return pl.ds(pl.multiple_of(k * piece, piece), piece)

    def scatter_copy(k, piece, src, dst, send, recv):
        target = lax.rem(me + k, n)
        return remote(
            src.at[span(target, piece)], dst.at[k - 1], send.at[k], recv.at[k], peer(k)
        )

    def scatter_a(k):
        return scatter_copy(k, piece_a, rs_a, rr_a, rs_send_a, rs_recv_a)

    def scatter_b(k):
        return scatter_copy(k, piece_b, rs_b, rr_b, rs_send_b, rs_recv_b)

    mate_a.wait()
    chip_a = part_a[core] + cr_a[...].astype(f32)
    part_a[core] = chip_a
    rs_a[...] = chip_a.astype(WIRE)
    each(n, lambda k: scatter_a(k).start())

    grad = contract(hid[...], d1[...], 0, 0)
    for c in range(nf):
        part_b[c, 0:hidden, :] = grad[:, c * half : (c + 1) * half]
    back = contract(d1[...], w1_ref[...], 1, 1).astype(bf16)
    small = jnp.concatenate(
        [
            contract(feat[...], back, 1, 0),
            contract(params_ref[...], back, 1, 0),
            grad_b2,
            grad_b1,
        ],
        axis=0,
    )
    used_b = hidden + levels + n_par + 2
    fill = jnp.zeros((nf, n * piece_b - used_b, half), f32)
    for c in range(nf):
        part_b[c, hidden:used_b, :] = small[:, c * half : (c + 1) * half]
    part_b[:, used_b:, :] = fill
    cs_b[...] = part_b[other].astype(WIRE)
    mate_b = remote(cs_b, cr_b, c_send.at[1], c_recv.at[1], mate)
    mate_b.start()
    gc_ref[...] = contract(proj_ref[...], back, 1, 1)

    mate_b.wait()
    chip_b = part_b[core] + cr_b[...].astype(f32)
    part_b[core] = chip_b
    rs_b[...] = chip_b.astype(WIRE)
    each(n, lambda k: scatter_b(k).start())

    def own_sum(piece, part, received, gathered):
        total = part[core, span(me, piece), :]
        if n <= 16:
            for k in range(1, n):
                total = total + received[k - 1].astype(f32)
        else:
            total = lax.fori_loop(
                1, n, lambda k, acc: acc + received[k - 1].astype(f32), total
            )
        gathered[core, span(me, piece), :] = (total * scale).astype(WIRE)

    def gathers(piece, buffer, send, recv, fsend, frecv):
        mine = buffer.at[core, span(me, piece)]

        def out(k):
            return remote(mine, mine, send.at[k], recv.at[k], peer(k))

        def forward(k):
            held = buffer.at[core, span(source(k), piece)]
            return remote(held, held, fsend.at[k], frecv.at[k], mate)

        return out, forward

    out_a, forward_a = gathers(piece_a, ag_a, ag_send_a, ag_recv_a, fw_send_a, fw_recv_a)
    out_b, forward_b = gathers(piece_b, ag_b, ag_send_b, ag_recv_b, fw_send_b, fw_recv_b)

    each(n, lambda k: scatter_a(k).wait())
    own_sum(piece_a, part_a, rr_a, ag_a)
    each(n, lambda k: out_a(k).start())
    forward_a(0).start()
    each(n, lambda k: scatter_b(k).wait())
    own_sum(piece_b, part_b, rr_b, ag_b)
    each(n, lambda k: out_b(k).start())
    forward_b(0).start()

    def pass_on(out, forward):
        def step(k):
            out(k).wait_recv()
            forward(k).start()

        each(n, step)

    pass_on(out_a, forward_a)
    forward_a(0).wait()
    each(n, lambda k: forward_a(k).wait())
    each(n, lambda k: out_a(k).wait_send())
    for c in range(nf):
        go_ref[c * half : (c + 1) * half, :] = ag_a[c, 0:half, :].astype(f32)
        gw2_ref[:, c * half : (c + 1) * half] = ag_a[c, half:used_a, :].astype(f32)

    pass_on(out_b, forward_b)
    forward_b(0).wait()
    each(n, lambda k: forward_b(k).wait())
    each(n, lambda k: out_b(k).wait_send())
    for c in range(nf):
        lanes = slice(c * half, (c + 1) * half)
        gw1_ref[:, lanes] = ag_b[c, 0:hidden, :].astype(f32)
        tail = ag_b[c, hidden:, :].astype(f32)
        gt_ref[:, lanes] = tail[0:levels]
        gp_ref[:, lanes] = tail[levels : levels + n_par]
        gb2_ref[:, lanes] = tail[levels + n_par : levels + n_par + 1]
        gb1_ref[:, lanes] = tail[levels + n_par + 1 : levels + n_par + 2]


def round_up(value, step):
    return -(-value // step) * step


def body(
    adjoint,
    target_x,
    target_y,
    target_z,
    assignment,
    level_codes,
    cell_params,
    level_table,
    w_proj,
    w_one,
    b_one,
    w_two,
    b_two,
    w_out,
):
    n = lax.axis_size("cells")
    nf = lax.axis_size("freq")
    cells = level_codes.shape[0]
    local = target_x.shape[0]
    hidden = w_one.shape[0]
    levels = level_table.shape[0]
    n_par = w_proj.shape[0]
    outs = w_out.shape[1]
    half = hidden // nf
    per = math.gcd(n, max(1, LANES // local))
    piece_a = round_up(-(-(half + hidden) // n), WIRE_ROWS)
    piece_b = round_up(-(-(hidden + levels + n_par + 2) // n), WIRE_ROWS)
    rows_a, rows_b = n * piece_a, n * piece_b
    scale = 1.0 / math.sqrt(cells * n * nf)
    vmem = pl.BlockSpec(memory_space=pltpu.VMEM)
    dma = pltpu.SemaphoreType.DMA
    results = pl.pallas_call(
        functools.partial(kernel, (n, nf, per, piece_a, piece_b, scale)),
        out_shape=[
            jax.ShapeDtypeStruct((hidden, outs), f32),
            jax.ShapeDtypeStruct((hidden, hidden), f32),
            jax.ShapeDtypeStruct((1, hidden), f32),
            jax.ShapeDtypeStruct((hidden, hidden), f32),
            jax.ShapeDtypeStruct((1, hidden), f32),
            jax.ShapeDtypeStruct((levels, hidden), f32),
            jax.ShapeDtypeStruct((n_par, hidden), f32),
            jax.ShapeDtypeStruct((n_par, cells), f32),
        ],
        in_specs=[vmem] * 14,
        out_specs=[vmem] * 8,
        scratch_shapes=[
            pltpu.VMEM((n, 8, per * local), f32),
            pltpu.VMEM((levels, cells), bf16),
            pltpu.VMEM((cells, hidden), bf16),
            pltpu.VMEM((cells, hidden), bf16),
            pltpu.VMEM((cells, hidden), f32),
            pltpu.VMEM((cells, hidden), bf16),
            pltpu.VMEM((cells, hidden), f32),
            pltpu.VMEM((cells, outs), bf16),
            pltpu.VMEM((cells, hidden), bf16),
            pltpu.VMEM((cells, hidden), bf16),
            pltpu.VMEM((nf, rows_a, half), f32),
            pltpu.VMEM((nf, rows_b, half), f32),
            pltpu.VMEM((rows_a, half), WIRE),
            pltpu.VMEM((rows_b, half), WIRE),
            pltpu.VMEM((rows_a, half), WIRE),
            pltpu.VMEM((rows_b, half), WIRE),
            pltpu.VMEM((rows_a, half), WIRE),
            pltpu.VMEM((rows_b, half), WIRE),
            pltpu.VMEM((n - 1, piece_a, half), WIRE),
            pltpu.VMEM((n - 1, piece_b, half), WIRE),
            pltpu.VMEM((nf, rows_a, half), WIRE),
            pltpu.VMEM((nf, rows_b, half), WIRE),
            dma((n,)),
            dma((n,)),
            dma((2,)),
            dma((2,)),
        ]
        + [dma((n,))] * 12,
        compiler_params=pltpu.CompilerParams(collective_id=0, has_side_effects=True),
        name="hologram_adjoint",
    )(
        adjoint,
        target_x[None, :],
        target_y[None, :],
        target_z[None, :],
        assignment[None, :],
        level_codes[None, :],
        cell_params,
        level_table,
        w_proj,
        w_one,
        b_one[None, :],
        w_two,
        b_two[None, :],
        w_out,
    )
    grad_out, grad_w2, grad_b2, grad_w1, grad_b1, grad_table, grad_proj, grad_params = results
    return (
        grad_out,
        grad_w2,
        grad_b2[0],
        grad_w1,
        grad_b1[0],
        grad_table,
        grad_proj,
        grad_params,
    )


def solution(mesh):
    placed = (
        P(None, ("groups", "cells")),
        P(("groups", "cells")),
        P(("groups", "cells")),
        P(("groups", "cells")),
        P(("groups", "cells")),
        P(("groups", "cells", "freq")),
        P(None, ("groups", "cells", "freq")),
        P(),
        P(),
        P(),
        P(),
        P(),
        P(),
        P(),
    )
    return jax.shard_map(
        body,
        mesh=mesh,
        in_specs=placed,
        out_specs=(
            P("groups", None),
            P("groups", None),
            P("groups"),
            P("groups", None),
            P("groups"),
            P("groups", None),
            P("groups", None),
            P(None, ("groups", "cells", "freq")),
        ),
        check_vma=False,
    )
```

time: 154 us -> 34.1 us (0.22)
  blocking collectives: 90.3 us -> 0 us
  waiting for transfers between devices: 34 us -> 0 us
  Pallas kernels: 0 us -> 27 us
  between operations: 14.2 us -> 0.67 us
  matrix products: 8.64 us -> 0 us
    psum x1 -> x0, blocking collectives: 57.9 us -> none  [body(): lax.psum((upper[0] * scale, upper[1] * scale, upper[2] * scale, lower[0]...]
    psum x1 -> x0, waiting for transfers between devices: 34 us -> none  [body(): lax.psum((upper[0] * scale, upper[1] * scale, upper[2] * scale, lower[0]...]
    all_gather x1 -> x0, blocking collectives: 32.4 us -> none  [body(): piece = lax.all_gather(stacked, 'cells', axis=1, tiled=True)]
    pallas_call x0 -> x1, Pallas kernels: none -> 27 us  [body(): pl.pallas_call(functools.partial(kernel, (n, nf, per, piece_a, piece_b, s...]
    dot_general x15 -> x0, matrix products: 8.64 us -> none  [the longest x12 7.85 us: contract(): lax.dot_general(left, right, (((left_dim,), (right_dim,)), ((), ())), pre...]
    unnamed x36 -> x22, local copies, waits for them, and re-layouts: 6.31 us -> 6.19 us
  transfers between devices with their start and end apart: 1 -> 0, of which waited for: 1 -> 0; matrix products, arithmetic and copies ran while one was open for 1% -> 0% of each run, Pallas kernels for 0% -> 0%
where the time goes in v1:
time: 34.1 us; the launch traced here: 33.8 us
  Pallas kernels  27 us (79%)
  local copies, waits for them, and re-layouts  6.19 us (18%)
  between operations  0.67 us (2%)
    pallas_call x1, Pallas kernels, body(): pl.pallas_call(functools.partial(kernel, (n, nf, per, piece_a, piece_b, s...  27 us
    unnamed x22, local copies, waits for them, and re-layouts  6.19 us

profile of v1, /device:TPU:0, one launch (start us, length us, event | category | flops | bytes accessed | tf_op | source)
XLA Modules:
  0.0 33.8 jit_solution(1063787513430207214)
XLA Ops:
  0.6 27.0 %hologram_adjoint.1 = (f32[256,128]{1,0:T(8,128)}, f32[256,256]{1,0:T(8,128)}, f32[1,256]{1,0:T(1,128)}, f32[256,256]{1,0:T(8,128)}, f32[1,256]{1,0:T(1,128)}, /...) custom-call(f32[2,16]{1,0:T(2,128)} %adj_ref.1, f32[1,16]{1,0:T(1,128)} %bitcast.14, f32[1,16]{1,0:T(1,128)} %bitcast.15, ...), custom_call_target="tpu_custom_call" | custom-call | tf_op jit(solution)/shard_map/hologram_adjoint/pallas_call | solution.py:423
  27.6 0.0 copy-start.1
  27.6 1.6 %copy.30 = f32[256,128]{1,0:T(8,128)} copy(f32[256,128]{1,0:T(8,128)} %get-tuple-element.32) | data formatting | bytes 262144
  29.3 0.0 copy-done.1
  29.3 0.0 copy-start.6
  29.3 0.0 copy-start
  29.3 0.7 %copy.31 = f32[256,256]{1,0:T(8,128)} copy(f32[256,256]{1,0:T(8,128)S(1)} %copy-done.1) | data formatting | bytes 524288
  30.0 0.0 copy-done.6
  30.0 0.6 %copy.32 = f32[256]{0:T(256)} copy(f32[256]{0:T(256)S(1)} %bitcast.13) | data formatting | bytes 2048
  30.5 0.0 copy-done
  30.5 0.0 copy-start.5
  30.5 0.0 copy-start.3
  30.5 0.7 %copy.33 = f32[256,256]{1,0:T(8,128)} copy(f32[256,256]{1,0:T(8,128)S(1)} %copy-done) | data formatting | bytes 524288
  31.2 0.0 copy-done.5
  31.2 0.6 %copy.34 = f32[256]{0:T(256)} copy(f32[256]{0:T(256)S(1)} %bitcast.12) | data formatting | bytes 2048
  31.8 0.0 copy-done.3
  31.8 0.0 copy-start.4
  31.8 0.6 %copy.35 = f32[16,256]{1,0:T(8,128)} copy(f32[16,256]{1,0:T(8,128)S(1)} %copy-done.3) | data formatting | bytes 32768
  32.4 0.1 copy-done.4
  32.5 0.0 copy-start.2
  32.5 0.6 %copy.36 = f32[8,256]{1,0:T(8,128)} copy(f32[8,256]{1,0:T(8,128)S(1)} %copy-done.4) | data formatting | bytes 16384
  33.1 0.1 copy-done.2
  33.2 0.6 %copy.37 = f32[8,512]{1,0:T(8,128)} copy(f32[8,512]{1,0:T(8,128)S(1)} %copy-done.2) | data formatting | bytes 32768
Async XLA Ops:
  27.6 1.6 %copy-start.1 = (f32[256,256]{1,0:T(8,128)S(1)}, f32[256,256]{1,0:T(8,128)}, u32[]{:S(2)}) copy-start(f32[256,256]{1,0:T(8,128)} %get-tuple-element.33) | copy-start | bytes 786436
  29.3 0.7 %copy-start.6 = (f32[1,256]{1,0:T(1,128)S(1)}, f32[1,256]{1,0:T(1,128)}, u32[]{:S(2)}) copy-start(f32[1,256]{1,0:T(1,128)} %get-tuple-element.18) | copy-start | bytes 3076
  29.3 1.3 %copy-start = (f32[256,256]{1,0:T(8,128)S(1)}, f32[256,256]{1,0:T(8,128)}, u32[]{:S(2)}) copy-start(f32[256,256]{1,0:T(8,128)} %get-tuple-element.35) | copy-start | bytes 786436
  30.5 0.7 %copy-start.5 = (f32[1,256]{1,0:T(1,128)S(1)}, f32[1,256]{1,0:T(1,128)}, u32[]{:S(2)}) copy-start(f32[1,256]{1,0:T(1,128)} %get-tuple-element.20) | copy-start | bytes 3076
  30.5 1.3 %copy-start.3 = (f32[16,256]{1,0:T(8,128)S(1)}, f32[16,256]{1,0:T(8,128)}, u32[]{:S(2)}) copy-start(f32[16,256]{1,0:T(8,128)} %get-tuple-element.37) | copy-start | bytes 49156
  31.8 0.7 %copy-start.4 = (f32[8,256]{1,0:T(8,128)S(1)}, f32[8,256]{1,0:T(8,128)}, u32[]{:S(2)}) copy-start(f32[8,256]{1,0:T(8,128)} %get-tuple-element.38) | copy-start | bytes 24580
  32.5 0.7 %copy-start.2 = (f32[8,512]{1,0:T(8,128)S(1)}, f32[8,512]{1,0:T(8,128)}, u32[]{:S(2)}) copy-start(f32[8,512]{1,0:T(8,128)} %get-tuple-element.39) | copy-start | bytes 49156

commit v2 on v1

--- a/solution.py
+++ b/solution.py
@@ -11,7 +11,8 @@
 SIDE = 1024
 LANES = 128
 WIRE = jnp.bfloat16
-WIRE_ROWS = 16
+WIRE_ROWS = 8
+VMEM_GRANT = 25165824
 
 wave_low = 1.0
 wave_high = 3.0
@@ -65,67 +66,68 @@
 
 def kernel(
     dims,
-    adj_ref,
-    x_ref,
-    y_ref,
-    z_ref,
-    asg_ref,
-    codes_ref,
-    params_ref,
-    table_ref,
-    proj_ref,
-    w1_ref,
-    b1_ref,
-    w2_ref,
-    b2_ref,
-    wo_ref,
-    go_ref,
-    gw2_ref,
-    gb2_ref,
-    gw1_ref,
-    gb1_ref,
-    gt_ref,
-    gp_ref,
-    gc_ref,
-    gath,
-    feat,
-    hid,
-    act1,
-    slope1,
-    act2,
-    slope2,
-    spec,
-    d2,
-    d1,
-    part_a,
-    part_b,
-    cs_a,
-    cs_b,
-    cr_a,
-    cr_b,
-    rs_a,
-    rs_b,
-    rr_a,
-    rr_b,
-    ag_a,
-    ag_b,
-    g_send,
-    g_recv,
-    c_send,
-    c_recv,
-    rs_send_a,
-    rs_recv_a,
-    rs_send_b,
-    rs_recv_b,
-    ag_send_a,
-    ag_recv_a,
-    ag_send_b,
-    ag_recv_b,
-    fw_send_a,
-    fw_recv_a,
-    fw_send_b,
-    fw_recv_b,
+    *refs,
 ):
+    inputs, results, loaded = refs[:14], refs[14:17], refs[17:31]
+    refs = results + refs[31:]
+    (
+        ag_a,
+        ag_b,
+        gc_ref,
+        gath,
+        feat,
+        hid,
+        act1,
+        slope1,
+        act2,
+        slope2,
+        spec,
+        d2,
+        d1,
+        part_a,
+        part_b,
+        cs_a,
+        cs_b,
+        cr_a,
+        cr_b,
+        rs_a,
+        rs_b,
+        rr_a,
+        rr_b,
+        g_send,
+        g_recv,
+        c_send,
+        c_recv,
+        rs_send_a,
+        rs_recv_a,
+        rs_send_b,
+        rs_recv_b,
+        ag_send_a,
+        ag_recv_a,
+        ag_send_b,
+        ag_recv_b,
+        fw_send_a,
+        fw_recv_a,
+        fw_send_b,
+        fw_recv_b,
+        load_sem,
+    ) = refs
+    (
+        adj_ref,
+        x_ref,
+        y_ref,
+        z_ref,
+        asg_ref,
+        codes_ref,
+        params_ref,
+        table_ref,
+        proj_ref,
+        w1_ref,
+        b1_ref,
+        w2_ref,
+        b2_ref,
+        wo_ref,
+    ) = loaded
     n, nf, per, piece_a, piece_b, scale = dims
     me = lax.axis_index("cells")
     core = lax.axis_index("freq")
@@ -166,6 +168,15 @@
     )
     pl.semaphore_signal(barrier, inc=1, device_id=mate, device_id_type=pl.DeviceIdType.MESH)
 
+    loads = [
+        pltpu.make_async_copy(src, dst, load_sem.at[i])
+        for i, (src, dst) in enumerate(zip(inputs, loaded))
+    ]
+    for load in loads:
+        load.start()
+    for load in loads[:5]:
+        load.wait()
+
     width = per * local
     rows = jnp.concatenate(
         [
@@ -184,6 +195,8 @@
     inside = jnp.logical_and(lane >= start, lane < start + local)
     gath[me] = jnp.where(inside, spread, 0.0)
 
+    for load in loads[5:11]:
+        load.wait()
     codes = codes_ref[...]
     onehot = (
         jnp.where(codes == lax.broadcasted_iota(jnp.int32, (levels, cells), 0), 1.0, 0.0)
@@ -204,6 +217,8 @@
 
     each(n, lambda k: gather_copy(k).start())
 
+    for load in loads[11:]:
+        load.wait()
     pre = contract(act1[...], w2_ref[...], 1, 0) + b2_ref[...]
     sig = 1.0 / (1.0 + jnp.exp(-pre))
     act2[...] = (pre * sig).astype(bf16)
@@ -366,22 +381,39 @@
     forward_a(0).wait()
     each(n, lambda k: forward_a(k).wait())
     each(n, lambda k: out_a(k).wait_send())
-    for c in range(nf):
-        go_ref[c * half : (c + 1) * half, :] = ag_a[c, 0:half, :].astype(f32)
-        gw2_ref[:, c * half : (c + 1) * half] = ag_a[c, half:used_a, :].astype(f32)
 
     pass_on(out_b, forward_b)
     forward_b(0).wait()
     each(n, lambda k: forward_b(k).wait())
     each(n, lambda k: out_b(k).wait_send())
+
+def unpack(
+    ag_a,
+    ag_b,
+    gc_in,
+    go_ref,
+    gw2_ref,
+    gb2_ref,
+    gw1_ref,
+    gb1_ref,
+    gt_ref,
+    gp_ref,
+    gc_ref,
+):
+    nf, _, half = ag_a.shape
+    hidden = gw2_ref.shape[0]
+    levels, n_par = gt_ref.shape[0], gp_ref.shape[0]
     for c in range(nf):
         lanes = slice(c * half, (c + 1) * half)
+        go_ref[lanes, :] = ag_a[c, 0:half, :].astype(f32)
+        gw2_ref[:, lanes] = ag_a[c, half : half + hidden, :].astype(f32)
         gw1_ref[:, lanes] = ag_b[c, 0:hidden, :].astype(f32)
         tail = ag_b[c, hidden:, :].astype(f32)
         gt_ref[:, lanes] = tail[0:levels]
         gp_ref[:, lanes] = tail[levels : levels + n_par]
         gb2_ref[:, lanes] = tail[levels + n_par : levels + n_par + 1]
         gb1_ref[:, lanes] = tail[levels + n_par + 1 : levels + n_par + 2]
+    gc_ref[...] = gc_in[...]
 
 
 def round_up(value, step):
@@ -420,21 +452,33 @@
     scale = 1.0 / math.sqrt(cells * n * nf)
     vmem = pl.BlockSpec(memory_space=pltpu.VMEM)
     dma = pltpu.SemaphoreType.DMA
-    results = pl.pallas_call(
+    args = (
+        adjoint,
+        target_x[None, :],
+        target_y[None, :],
+        target_z[None, :],
+        assignment[None, :],
+        level_codes[None, :],
+        cell_params,
+        level_table,
+        w_proj,
+        w_one,
+        b_one[None, :],
+        w_two,
+        b_two[None, :],
+        w_out,
+    )
+    packed = pl.pallas_call(
         functools.partial(kernel, (n, nf, per, piece_a, piece_b, scale)),
         out_shape=[
-            jax.ShapeDtypeStruct((hidden, outs), f32),
-            jax.ShapeDtypeStruct((hidden, hidden), f32),
-            jax.ShapeDtypeStruct((1, hidden), f32),
-            jax.ShapeDtypeStruct((hidden, hidden), f32),
-            jax.ShapeDtypeStruct((1, hidden), f32),
-            jax.ShapeDtypeStruct((levels, hidden), f32),
-            jax.ShapeDtypeStruct((n_par, hidden), f32),
-            jax.ShapeDtypeStruct((n_par, cells), f32),
+            pltpu.VMEM((nf, rows_a, half), WIRE),
+            pltpu.VMEM((nf, rows_b, half), WIRE),
+            pltpu.VMEM((n_par, cells), f32),
         ],
-        in_specs=[vmem] * 14,
-        out_specs=[vmem] * 8,
-        scratch_shapes=[
+        in_specs=[pl.BlockSpec(memory_space=pltpu.HBM)] * 14,
+        out_specs=[vmem] * 3,
+        scratch_shapes=[pltpu.VMEM(arg.shape, arg.dtype) for arg in args]
+        + [
             pltpu.VMEM((n, 8, per * local), f32),
             pltpu.VMEM((levels, cells), bf16),
             pltpu.VMEM((cells, hidden), bf16),
@@ -455,32 +499,35 @@
             pltpu.VMEM((rows_b, half), WIRE),
             pltpu.VMEM((n - 1, piece_a, half), WIRE),
             pltpu.VMEM((n - 1, piece_b, half), WIRE),
-            pltpu.VMEM((nf, rows_a, half), WIRE),
-            pltpu.VMEM((nf, rows_b, half), WIRE),
             dma((n,)),
             dma((n,)),
             dma((2,)),
             dma((2,)),
         ]
-        + [dma((n,))] * 12,
-        compiler_params=pltpu.CompilerParams(collective_id=0, has_side_effects=True),
+        + [dma((n,))] * 12
+        + [dma((len(args),))],
+        compiler_params=pltpu.CompilerParams(
+            collective_id=0, has_side_effects=True, vmem_limit_bytes=VMEM_GRANT
+        ),
         name="hologram_adjoint",
-    )(
-        adjoint,
-        target_x[None, :],
-        target_y[None, :],
-        target_z[None, :],
-        assignment[None, :],
-        level_codes[None, :],
-        cell_params,
-        level_table,
-        w_proj,
-        w_one,
-        b_one[None, :],
-        w_two,
-        b_two[None, :],
-        w_out,
-    )
+    )(*[pltpu.with_memory_space_constraint(arg, pltpu.HBM) for arg in args])
+    results = pl.pallas_call(
+        unpack,
+        out_shape=[
+            jax.ShapeDtypeStruct((hidden, outs), f32),
+            jax.ShapeDtypeStruct((hidden, hidden), f32),
+            jax.ShapeDtypeStruct((1, hidden), f32),
+            jax.ShapeDtypeStruct((hidden, hidden), f32),
+            jax.ShapeDtypeStruct((1, hidden), f32),
+            jax.ShapeDtypeStruct((levels, hidden), f32),
+            jax.ShapeDtypeStruct((n_par, hidden), f32),
+            jax.ShapeDtypeStruct((n_par, cells), f32),
+        ],
+        in_specs=[vmem] * 3,
+        out_specs=[vmem] * 8,
+        compiler_params=pltpu.CompilerParams(vmem_limit_bytes=VMEM_GRANT),
+        name="unpack",
+    )(*packed)
     grad_out, grad_w2, grad_b2, grad_w1, grad_b1, grad_table, grad_proj, grad_params = results
     return (
         grad_out,

time: 34.1 us -> 26.6 us (0.78)
  local copies, waits for them, and re-layouts: 6.19 us -> 0 us
  Pallas kernels: 27 us -> 25.8 us
    unnamed x22 -> x0, local copies, waits for them, and re-layouts: 6.19 us -> none
    pallas_call x1, Pallas kernels: 27 us -> 24.9 us  [body(): pl.pallas_call(functools.partial(kernel, (n, nf, per, piece_a, piece_b, s...]
    pallas_call x0 -> x1, Pallas kernels: none -> 0.88 us  [body(): pl.pallas_call(unpack, out_shape=[jax.ShapeDtypeStruct((hidden, outs), f3...]
where the time goes in v2:
time: 26.6 us; the launch traced here: 26.4 us
  Pallas kernels  25.8 us (97%)
  between operations  0.65 us (2%)
    pallas_call x1, Pallas kernels, body(): pl.pallas_call(functools.partial(kernel, (n, nf, per, piece_a, piece_b, s...  24.9 us
    pallas_call x1, Pallas kernels, body(): pl.pallas_call(unpack, out_shape=[jax.ShapeDtypeStruct((hidden, outs), f3...  0.88 us

profile of v2, /device:TPU:0, one launch (start us, length us, event | category | flops | bytes accessed | tf_op | source)
XLA Modules:
  0.0 26.4 jit_solution(3694770889395235347)
XLA Ops:
  0.6 24.9 %hologram_adjoint.1 = (bf16[2,384,128]{2,1,0:T(8,128)(2,1)S(1)}, bf16[2,320,128]{2,1,0:T(8,128)(2,1)S(1)}, f32[8,512]{1,0:T(8,128)S(1)}) custom-call(f32[2,16]{1,0:T(2,128)} %refs_0_.1, f32[1,16]{1,0:T(1,128)} %bitcast.12, f32[1,16]{1,0:T(1,128)} %bitcast.13, f32[1,16]{1,0:T(1,128)} %bitcast.14, s32[1,16]{1,0:T(1,128)} %bitcast.15, s32[1,512]{1,0:T(1,128)} %bitcast.9, ...), custom_call_target="tpu_custom_call" | custom-call | tf_op jit(solution)/shard_map/hologram_adjoint/pallas_call | solution.py:471
  25.5 0.9 %unpack.1 = (f32[256,128]{1,0:T(8,128)}, f32[256,256]{1,0:T(8,128)}, f32[1,256]{1,0:T(1,128)}, f32[256,256]{1,0:T(8,128)}, f32[1,256]{1,0:T(1,128)}, /*index=5*/...) custom-call(bf16[2,384,128]{2,1,0:T(8,128)(2,1)S(1)} %get-tuple-element.19.ag_a, ...), custom_call_target="tpu_custom_call" | custom-call | tf_op jit(solution)/shard_map/unpack/pallas_call | solution.py:514
